TPU v7x, 512 devices: a whole 4x4x16 slice. The times are simulated.
512 devices in a mesh: dp: 32 (over z, core), tensor: 16 (over y, x).
Axes of the slice: x: 4, y: 4, z: 16, core: 2. Of those that a mesh axis runs over, the one named last changes fastest.
Arguments:
- dout: bfloat16 [12288, 5120], P(('dp', 'tensor')), may hold values from -0.75 to 0.75
- attn_ctx: bfloat16 [12288, 5120], P('dp', 'tensor'), may hold values from -6 to 6
- mlp_hidden: bfloat16 [12288, 13824], P('dp', 'tensor'), may hold values from -6 to 6
- w_out: bfloat16 [5120, 5120], P('tensor', 'dp'), may hold values from -0.078125 to 0.078125
- w_down: bfloat16 [13824, 5120], P('tensor', 'dp'), may hold values from -0.0546875 to 0.0546875
- head_logits: float32 [40], replicated, may hold values from -2 to 3
- unit_logits: float32 [13824], P('tensor'), may hold values from -2 to 3
- head_noise: float32 [40], replicated, may hold values from 0.001 to 0.999
- unit_noise: float32 [13824], P('tensor'), may hold values from 0.001 to 0.999
- linear_mult: float32 [1], replicated, may hold values from 100 to 300
- square_mult: float32 [1], replicated, may hold values from 1 to 4
- target: float32 [1], replicated, may hold values from 40 to 70
Outputs:
- ctx_grad: bfloat16 [12288, 5120], P('dp', 'tensor')
- hidden_grad: bfloat16 [12288, 13824], P('dp', 'tensor')
- head_grad: float32 [40], replicated
- unit_grad: float32 [13824], P('tensor')
All inputs are finite; a program needn't handle non-finite values.
Results may differ from a plain program's by a relative error of at most 0.001.
Values may be sent and summed in bfloat16 or wider, within the bound.
No kernel may reach another device: no remote copies, remote signals or barrier semaphores. Data moves between devices by JAX's collectives and lax.ppermute only.
A program may use at most 64 MiB of HBM per device.

v0:
```python
import jax
import jax.numpy as jnp
from jax import lax
from jax.sharding import PartitionSpec as P

H = 40
HEAD = 128
FF = 13824
low_end = -0.1
high_end = 1.1
temper = 2.0 / 3.0


def concrete(logits, noise):
    shape_s = jax.nn.sigmoid((jnp.log(noise) - jnp.log(1.0 - noise) + logits) / temper)
    stretched = shape_s * (high_end - low_end) + low_end
    gate = jnp.clip(stretched, 0.0, 1.0)
    inside = jnp.logical_and(stretched > 0.0, stretched < 1.0)
    slope = jnp.where(
        inside, (high_end - low_end) / temper * shape_s * (1.0 - shape_s), 0.0 * shape_s
    )
    return (gate, slope)


def open_prob(logits):
    return jax.nn.sigmoid(logits - temper * jnp.log(-low_end / high_end))


def local(
    dout,
    attn_ctx,
    mlp_hidden,
    w_out,
    w_down,
    head_logits,
    unit_logits,
    head_noise,
    unit_noise,
    linear_mult,
    square_mult,
    target,
):
    head_gate, head_slope = concrete(head_logits, head_noise)
    unit_gate, unit_slope = concrete(unit_logits, unit_noise)
    col_count = attn_ctx.shape[1]
    head_total = head_logits.shape[0]
    tensor_index = lax.axis_index("tensor")
    columns = tensor_index * col_count + lax.iota(jnp.int32, col_count)
    owner = columns // HEAD
    member = (owner[:, None] == lax.iota(jnp.int32, head_total)[None, :]).astype(jnp.float32)
    col_gate = jnp.dot(member, head_gate, precision=lax.Precision.HIGHEST)
    full_rows = lax.all_gather(dout, "tensor", axis=0, tiled=True)
    dims = (((1,), (1,)), ((), ()))

    def contract(piece):
        return lax.dot_general(full_rows, piece, dims, preferred_element_type=jnp.float32)

    ctx_pre = contract(lax.all_gather(w_out, "dp", axis=1, tiled=True))
    hid_pre = contract(lax.all_gather(w_down, "dp", axis=1, tiled=True))
    ctx_grad = (ctx_pre * col_gate[None, :]).astype(jnp.bfloat16)
    hidden_grad = (hid_pre * unit_gate[None, :]).astype(jnp.bfloat16)
    col_part = jnp.sum(attn_ctx.astype(jnp.float32) * ctx_pre, axis=0)
    unit_part = jnp.sum(mlp_hidden.astype(jnp.float32) * hid_pre, axis=0)
    head_part = jnp.dot(col_part, member, precision=lax.Precision.HIGHEST)
    p_head = open_prob(head_logits)
    p_unit = open_prob(unit_logits)
    local_mass = jnp.sum(p_unit)
    unit_data = lax.psum(unit_part, "dp")
    head_data = lax.psum(head_part, ("dp", "tensor"))
    unit_mass = lax.psum(local_mass, "tensor")
    denom = 4.0 * HEAD * H + 3.0 * FF
    size = 100.0 * (4.0 * HEAD * jnp.sum(p_head) + 3.0 * unit_mass) / denom
    factor = linear_mult[0] + 2.0 * square_mult[0] * (size - target[0])
    head_grad = head_data * head_slope + factor * (400.0 * HEAD / denom) * p_head * (1.0 - p_head)
    unit_grad = unit_data * unit_slope + factor * (300.0 / denom) * p_unit * (1.0 - p_unit)
    return (ctx_grad, hidden_grad, head_grad, unit_grad)


def solution(mesh):
    placed = (
        P(("dp", "tensor"), None),
        P("dp", "tensor"),
        P("dp", "tensor"),
        P("tensor", "dp"),
        P("tensor", "dp"),
        P(),
        P("tensor"),
        P(),
        P("tensor"),
        P(),
        P(),
        P(),
    )
    return jax.shard_map(
        local,
        mesh=mesh,
        in_specs=placed,
        out_specs=(P("dp", "tensor"), P("dp", "tensor"), P(), P("tensor")),
        check_vma=False,
    )
```

profile of v0, /device:TPU:1, one launch (start us, length us, event | category | flops | bytes accessed | tf_op | source)
XLA Modules:
  0.0 329.6 jit_solution(5489138382124432926)
XLA Ops:
  7.2 0.0 all-gather.6.cloned.1.call-start
  7.2 0.7 all-gather.6.cloned.1.call-update
  7.9 0.0 all-gather.4.cloned.1.call-start
  7.9 0.7 all-gather.4.cloned.1.call-update
  8.6 0.0 all-gather.8.cloned.1.call-start
  8.7 0.7 all-gather.8.cloned.1.call-update
  9.4 1.3 fusion.2
  10.7 34.9 %psum.22 = f32[]{:T(128)} all-reduce(f32[]{:T(128)} %get-tuple-element.11), channel_id=1, replica_groups=mesh['dp'=32,'tensor'=16] {'tensor'}, use_global_device_ids=true, to_apply=%region_4.5 | all-reduce | flops 1 | bytes 8 | tf_op jit(solution)/shard_map/psum | solution.py:70
  48.2 1.3 fusion.17
  50.1 0.0 copy-start.2
  50.1 0.0 copy-start.3
  50.2 0.0 copy-start.4
  50.2 38.7 %all-gather.6.cloned.1.call-done = bf16[320,5120]{0,1:T(8,128)(2,1)} async-done(((bf16[320,160]{0,1:T(8,128)(2,1)}), bf16[320,5120]{0,1:T(8,128)(2,1)}) %all-gather.6.cloned.1.call-update) | async-done | bytes 3276816 | tf_op jit(solution)/shard_map/all_gather | solution.py:58
  88.8 65.0 %all-gather.4.cloned.1.call-done = bf16[384,5120]{1,0:T(8,128)(2,1)} async-done(((bf16[24,5120]{1,0:T(8,128)(2,1)}), bf16[384,5120]{1,0:T(8,128)(2,1)}) %all-gather.4.cloned.1.call-update) | async-done | bytes 3932176 | tf_op jit(solution)/shard_map/all_gather | solution.py:52
  153.9 5.3 %multiply_reduce_fusion.1 = (f32[320]{0:T(512)S(1)}, f32[384,320]{0,1:T(8,128)S(1)}) fusion(bf16[384,320]{0,1:T(8,128)(2,1)} %param.13, bf16[384,5120]{1,0:T(8,128)(2,1)} %all-gather.4.cloned.1.call-done, bf16[320,5120]{0,1:T(8,128)(2,1)} %all-gather.6.cloned.1.call-done), kind=kOutput, calls=%fused_computation.4 | convolution fusion | flops 1258659584 | bytes 7947520 | tf_op jit(solution)/shard_map/dot_general | solution.py:56
  159.2 0.2 convolution_bitcast_fusion
  159.5 105.0 %psum.21 = f32[40]{0:T(128)S(1)} all-reduce(f32[40]{0:T(128)S(1)} %convolution_bitcast_fusion), channel_id=1, replica_groups=mesh['dp'=32,'tensor'=16] {'dp','tensor'}, use_global_device_ids=true, to_apply=%region_1.2 | all-reduce | flops 40 | bytes 320 | tf_op jit(solution)/shard_map/psum | solution.py:69
  264.5 0.0 copy-done.2
  264.5 0.0 copy-done.3
  264.5 0.5 multiply_add_fusion.2
  265.0 0.3 convolution_reduce_fusion
  265.3 0.8 multiply_convert_fusion.1
  266.1 0.0 all-gather.8.cloned.1.call-done
  266.2 0.0 copy-done.4
  266.2 0.0 copy-start
  266.2 0.0 copy-start.1
  266.2 10.5 %multiply_reduce_fusion = (f32[864]{0:T(1024)S(1)}, bf16[384,864]{0,1:T(8,128)(2,1)}) fusion(bf16[384,864]{0,1:T(8,128)(2,1)S(1)} %copy-done.4, f32[864]{0:T(1024)S(1)} %get-tuple-element.10, bf16[384,5120]{1,0:T(8,128)(2,1)} %all-gather.4.cloned.1.call-done, bf16[864,5120]{0,1:T(8,128)(2,1)} %all-gather.8.cloned.1.call-done), kind=kOutput, calls=%fused_computation | convolution fusion | flops 3399044352 | bytes 14113536 | tf_op jit(solution)/shard_map/dot_general | solution.py:56
  276.7 45.8 %psum.23 = f32[864]{0:T(1024)S(1)} all-reduce(f32[864]{0:T(1024)S(1)} %get-tuple-element.8), channel_id=1, replica_groups=mesh['dp'=32,'tensor'=16] {'dp'}, use_global_device_ids=true, to_apply=%region_6.7 | all-reduce | flops 864 | bytes 6912 | tf_op jit(solution)/shard_map/psum | solution.py:68
  322.5 0.0 copy-done
  322.5 0.0 copy-done.1
  322.5 0.6 multiply_add_fusion
  (2 shorter events, 0.0 us)
Async XLA Ops:
  7.2 81.7 %all-gather.6.cloned.1.call-start = ((), (), s32[]{:S(2)}) async-start(), calls=%async_computation.1 | async-start | bytes 4055040 | tf_op jit(solution)/shard_map/all_gather | solution.py:58
  7.9 146.0 %all-gather.4.cloned.1.call-start = ((), (), s32[]{:S(2)}) async-start(), calls=%async_computation | async-start | bytes 4177920 | tf_op jit(solution)/shard_map/all_gather | solution.py:52
  8.6 257.5 %all-gather.8.cloned.1.call-start = ((), (), s32[]{:S(2)}) async-start(), calls=%async_computation.2 | async-start | bytes 9461760 | tf_op jit(solution)/shard_map/all_gather | solution.py:59
  50.1 214.4 %copy-start.2 = (f32[40]{0:T(128)S(1)}, f32[40]{0:T(128)}, u32[]{:S(2)}) copy-start(f32[40]{0:T(128)} %param.17) | copy-start | bytes 484
  50.1 214.4 %copy-start.3 = (f32[40]{0:T(128)S(1)}, f32[40]{0:T(128)}, u32[]{:S(2)}) copy-start(f32[40]{0:T(128)} %param.19) | copy-start | bytes 484
  50.2 216.0 %copy-start.4 = (bf16[384,864]{0,1:T(8,128)(2,1)S(1)}, bf16[384,864]{0,1:T(8,128)(2,1)}, u32[]{:S(2)}) copy-start(bf16[384,864]{0,1:T(8,128)(2,1)} %param.14) | copy-start | bytes 1990660
  266.2 56.3 %copy-start = (f32[864]{0:T(1024)S(1)}, f32[864]{0:T(1024)}, u32[]{:S(2)}) copy-start(f32[864]{0:T(1024)} %param.18) | copy-start | bytes 10372
  266.2 56.3 %copy-start.1 = (f32[864]{0:T(1024)S(1)}, f32[864]{0:T(1024)}, u32[]{:S(2)}) copy-start(f32[864]{0:T(1024)} %param.20) | copy-start | bytes 10372
Sparse Core Ops, SparseCore 0:
  10.1 78.6 all-gather.5
  91.8 61.9 all-gather.3
  156.0 80.5 all-gather.7
where the time goes:
time: 330 us
  blocking collectives  186 us (56%)
  waiting for transfers between devices  106 us (32%)
  between operations  17.1 us (5%)
  matrix products  16.4 us (5%)
  other arithmetic  4.6 us (1%)
    psum x1, blocking collectives, local(): head_data = lax.psum(head_part, ('dp', 'tensor'))  105 us
    all_gather x1, waiting for transfers between devices, local(): full_rows = lax.all_gather(dout, 'tensor', axis=0, tiled=True)  65 us
    psum x1, blocking collectives, local(): unit_data = lax.psum(unit_part, 'dp')  45.8 us
    all_gather x1, waiting for transfers between devices, local(): ctx_pre = contract(lax.all_gather(w_out, 'dp', axis=1, tiled=True))  38.7 us
    psum x1, blocking collectives, local(): unit_mass = lax.psum(local_mass, 'tensor')  34.9 us
    dot_general x2, matrix products, contract(): lax.dot_general(full_rows, piece, dims, preferred_element_type=jnp.float32)  15.9 us
  transfers between devices with their start and end apart: 3, of which 2 were waited for; matrix products, arithmetic and copies ran while one was open for 3% of the time, Pallas kernels for 0%

commit v1 on v0

--- a/solution.py
+++ b/solution.py
@@ -9,6 +9,13 @@
 low_end = -0.1
 high_end = 1.1
 temper = 2.0 / 3.0
+
+
+def _refer_view(z_in, mesh_ax, axis_no):
+    tile_out = lax.axis_size(mesh_ax)
+    current_value = jnp.stack([z_in] * tile_out, 0)
+    val2 = lax.all_to_all(current_value, axis_name=mesh_ax, split_axis=0, concat_axis=0)
+    return jnp.concatenate(val2, axis_no)
 
 
 def concrete(logits, noise):
@@ -55,7 +62,7 @@
     def contract(piece):
         return lax.dot_general(full_rows, piece, dims, preferred_element_type=jnp.float32)
 
-    ctx_pre = contract(lax.all_gather(w_out, "dp", axis=1, tiled=True))
+    ctx_pre = contract(_refer_view(w_out, mesh_ax="dp", axis_no=1))
     hid_pre = contract(lax.all_gather(w_down, "dp", axis=1, tiled=True))
     ctx_grad = (ctx_pre * col_gate[None, :]).astype(jnp.bfloat16)
     hidden_grad = (hid_pre * unit_gate[None, :]).astype(jnp.bfloat16)

time: 330 us -> 408 us (1.24)
  waiting for transfers between devices: 106 us -> 166 us
  starting transfers between devices: 0.11 us -> 17 us
    all_to_all x0 -> x1, waiting for transfers between devices: none -> 152 us  [_refer_view(): lax.all_to_all(current_value, axis_name=mesh_ax, split_axis=0, concat_axi...]
    all_gather x1, waiting for transfers between devices: 65 us -> 11.9 us  [local(): full_rows = lax.all_gather(dout, 'tensor', axis=0, tiled=True)]
    all_gather x1 -> x0, waiting for transfers between devices: 38.7 us -> none  [local(): ctx_pre = contract(lax.all_gather(w_out, 'dp', axis=1, tiled=True))]
    all_to_all x0 -> x1, starting transfers between devices: none -> 16.9 us  [_refer_view(): lax.all_to_all(current_value, axis_name=mesh_ax, split_axis=0, concat_axi...]
where the time goes in v1:
time: 408 us
  blocking collectives  185 us (45%)
  waiting for transfers between devices  166 us (41%)
  between operations  17.4 us (4%)
  starting transfers between devices  17 us (4%)
  matrix products  16.6 us (4%)
    all_to_all x1, waiting for transfers between devices, _refer_view(): lax.all_to_all(current_value, axis_name=mesh_ax, split_axis=0, concat_axi...  152 us
    psum x1, blocking collectives, local(): head_data = lax.psum(head_part, ('dp', 'tensor'))  102 us
    psum x1, blocking collectives, local(): unit_data = lax.psum(unit_part, 'dp')  46.1 us
    psum x1, blocking collectives, local(): unit_mass = lax.psum(local_mass, 'tensor')  36.5 us
    all_to_all x1, starting transfers between devices, _refer_view(): lax.all_to_all(current_value, axis_name=mesh_ax, split_axis=0, concat_axi...  16.9 us
    dot_general x2, matrix products, contract(): lax.dot_general(full_rows, piece, dims, preferred_element_type=jnp.float32)  16 us
    all_gather x1, waiting for transfers between devices, local(): full_rows = lax.all_gather(dout, 'tensor', axis=0, tiled=True)  11.9 us
  transfers between devices with their start and end apart: 3, of which 2 were waited for; matrix products, arithmetic and copies ran while one was open for 3% of the time, Pallas kernels for 0%

profile of v1, /device:TPU:1, one launch (start us, length us, event | category | flops | bytes accessed | tf_op | source)
XLA Modules:
  0.0 407.8 jit_solution(17957573160274445598)
XLA Ops:
  7.2 0.0 all-gather.3.cloned.1.call-start
  7.2 0.7 all-gather.3.cloned.1.call-update
  7.9 0.0 all-gather.5.cloned.1.call-start
  7.9 0.7 all-gather.5.cloned.1.call-update
  8.6 3.1 stack.2
  11.7 0.0 copy-start
  11.7 0.0 copy-start.1
  11.7 0.0 copy-start.2
  11.7 0.0 copy-start.5
  11.7 16.9 %all-to-all-start = ((bf16[32,320,160]{1,2,0:T(8,128)(2,1)}), bf16[32,320,160]{1,2,0:T(8,128)(2,1)}, u32[]{:S(2)}, u32[]{:S(2)}) async-start(bf16[32,320,160]{1,2,0:T(8,128)(2,1)} %stack.2), calls=%async_computation | async-start | bytes 7864320 | tf_op jit(solution)/shard_map/all_to_all | solution.py:17
  28.7 0.0 copy-done
  28.7 0.0 copy-done.1
  28.7 0.6 fusion.2
  29.3 36.5 %psum.22 = f32[]{:T(128)} all-reduce(f32[]{:T(128)} %get-tuple-element.11), channel_id=1, replica_groups=mesh['dp'=32,'tensor'=16] {'tensor'}, use_global_device_ids=true, to_apply=%region_4.5 | all-reduce | flops 1 | bytes 8 | tf_op jit(solution)/shard_map/psum | solution.py:77
  67.8 0.0 copy-done.2
  67.8 0.6 fusion.17
  69.8 11.9 %all-gather.3.cloned.1.call-done = bf16[384,5120]{1,0:T(8,128)(2,1)} async-done(((bf16[24,5120]{1,0:T(8,128)(2,1)}), bf16[384,5120]{1,0:T(8,128)(2,1)}) %all-gather.3.cloned.1.call-update) | async-done | bytes 3932176 | tf_op jit(solution)/shard_map/all_gather | solution.py:59
  81.6 152.3 %all-to-all-done = bf16[32,320,160]{1,2,0:T(8,128)(2,1)} async-done(((bf16[32,320,160]{1,2,0:T(8,128)(2,1)}), bf16[32,320,160]{1,2,0:T(8,128)(2,1)}, u32[]{:S(2)}, u32[]{:S(2)}) %all-to-all-start) | async-done | bytes 3276832 | tf_op jit(solution)/shard_map/all_to_all | solution.py:17
  234.0 0.0 copy-done.5
  234.0 0.0 copy-start.3
  234.0 0.0 copy-start.4
  234.0 5.6 %multiply_reduce_fusion.1 = (f32[320]{0:T(512)S(1)}, f32[384,320]{0,1:T(8,128)S(1)}) fusion(bf16[384,320]{0,1:T(8,128)(2,1)S(1)} %copy-done.5, bf16[384,5120]{1,0:T(8,128)(2,1)} %all-gather.3.cloned.1.call-done, bf16[320,5120]{0,1:T(8,128)(2,1)} %bitcast.1), kind=kOutput, calls=%fused_computation.4 | convolution fusion | flops 1258659584 | bytes 7947520 | tf_op jit(solution)/shard_map/dot_general | solution.py:63
  239.5 0.2 convolution_bitcast_fusion
  239.8 102.3 %psum.21 = f32[40]{0:T(128)S(1)} all-reduce(f32[40]{0:T(128)S(1)} %convolution_bitcast_fusion), channel_id=1, replica_groups=mesh['dp'=32,'tensor'=16] {'dp','tensor'}, use_global_device_ids=true, to_apply=%region_1.2 | all-reduce | flops 40 | bytes 320 | tf_op jit(solution)/shard_map/psum | solution.py:76
  342.1 0.0 copy-done.3
  342.1 0.5 multiply_add_fusion.2
  342.6 0.3 convolution_reduce_fusion
  342.9 0.8 multiply_convert_fusion.1
  343.7 0.0 copy-done.4
  343.7 10.5 %multiply_reduce_fusion = (f32[864]{0:T(1024)S(1)}, bf16[384,864]{0,1:T(8,128)(2,1)}) fusion(bf16[384,864]{0,1:T(8,128)(2,1)S(1)} %copy-done.4, f32[864]{0:T(1024)S(1)} %get-tuple-element.10, bf16[384,5120]{1,0:T(8,128)(2,1)} %all-gather.3.cloned.1.call-done, bf16[864,5120]{0,1:T(8,128)(2,1)} %all-gather.5.cloned.1.call-done), kind=kOutput, calls=%fused_computation | convolution fusion | flops 3399044352 | bytes 14113536 | tf_op jit(solution)/shard_map/dot_general | solution.py:63
  354.2 46.1 %psum.23 = f32[864]{0:T(1024)S(1)} all-reduce(f32[864]{0:T(1024)S(1)} %get-tuple-element.8), channel_id=1, replica_groups=mesh['dp'=32,'tensor'=16] {'dp'}, use_global_device_ids=true, to_apply=%region_6.7 | all-reduce | flops 864 | bytes 6912 | tf_op jit(solution)/shard_map/psum | solution.py:75
  400.3 0.6 multiply_add_fusion
  (3 shorter events, 0.0 us)
Async XLA Ops:
  7.2 74.5 %all-gather.3.cloned.1.call-start = ((), (), s32[]{:S(2)}) async-start(), calls=%async_computation.1 | async-start | bytes 4177920 | tf_op jit(solution)/shard_map/all_gather | solution.py:59
  7.9 335.8 %all-gather.5.cloned.1.call-start = ((), (), s32[]{:S(2)}) async-start(), calls=%async_computation.2 | async-start | bytes 9461760 | tf_op jit(solution)/shard_map/all_gather | solution.py:66
  11.7 17.0 %copy-start = (f32[864]{0:T(1024)S(1)}, f32[864]{0:T(1024)}, u32[]{:S(2)}) copy-start(f32[864]{0:T(1024)} %param.18) | copy-start | bytes 10372
  11.7 17.0 %copy-start.1 = (f32[864]{0:T(1024)S(1)}, f32[864]{0:T(1024)}, u32[]{:S(2)}) copy-start(f32[864]{0:T(1024)} %param.20) | copy-start | bytes 10372
  11.7 56.1 %copy-start.2 = (f32[40]{0:T(128)S(1)}, f32[40]{0:T(128)}, u32[]{:S(2)}) copy-start(f32[40]{0:T(128)} %param.17) | copy-start | bytes 484
  11.7 222.2 %copy-start.5 = (bf16[384,320]{0,1:T(8,128)(2,1)S(1)}, bf16[384,320]{0,1:T(8,128)(2,1)}, u32[]{:S(2)}) copy-start(bf16[384,320]{0,1:T(8,128)(2,1)} %param.13) | copy-start | bytes 737284
  11.7 222.2 %all-to-all-start = ((bf16[32,320,160]{1,2,0:T(8,128)(2,1)}), bf16[32,320,160]{1,2,0:T(8,128)(2,1)}, u32[]{:S(2)}, u32[]{:S(2)}) async-start(bf16[32,320,160]{1,2,0:T(8,128)(2,1)} %stack.2), calls=%async_computation | async-start | bytes 7864320 | tf_op jit(solution)/shard_map/all_to_all | solution.py:17
  234.0 108.1 %copy-start.3 = (f32[40]{0:T(128)S(1)}, f32[40]{0:T(128)}, u32[]{:S(2)}) copy-start(f32[40]{0:T(128)} %param.19) | copy-start | bytes 484
  234.0 109.7 %copy-start.4 = (bf16[384,864]{0,1:T(8,128)(2,1)S(1)}, bf16[384,864]{0,1:T(8,128)(2,1)}, u32[]{:S(2)}) copy-start(bf16[384,864]{0,1:T(8,128)(2,1)} %param.14) | copy-start | bytes 1990660
Sparse Core Ops, SparseCore 0:
  11.0 70.6 all-gather.2
  83.8 171.4 all-gather.4
